TPU v7x, 256 devices: a whole 4x4x8 slice. The times are simulated.
256 devices in a mesh: tm: 8 (over z), height: 16 (over x, y), width: 2 (over core).
Axes of the slice: x: 4, y: 4, z: 8, core: 2. Of those that a mesh axis runs over, the one named last changes fastest.
Arguments:
- video: bfloat16 [2, 128, 16, 256, 128], P('width', ('tm', 'height')), may hold values from -6 to 6
- out_grad: bfloat16 [2, 128, 16, 256, 128], P('width', None, 'tm', 'height'), may hold values from -6 to 6
- lengths: int32 [4], replicated, may hold values from 1 to 6, 16 in all
- temporal_weight: bfloat16 [3, 128, 128], replicated, may hold values from -0.3125 to 0.3125
- spatial_weight: bfloat16 [3, 3, 128, 128], replicated, may hold values from -0.1875 to 0.1875
Outputs:
- video_grad: bfloat16 [2, 128, 16, 256, 128], P('width', ('tm', 'height'))
- temporal_grad: float32 [3, 128, 128], replicated
- spatial_grad: float32 [3, 3, 128, 128], replicated
Inputs may be any that keep to these rules, and one draw needn't show every extreme that they name: The 4 clips lie end to end in frame order, their lengths sum to 16, and the longest clip has exactly 6 frames.
All inputs are finite; a program needn't handle non-finite values.
Results may differ from a plain program's by a relative error of at most 0.008.
Values may be sent and summed in bfloat16 or wider, within the bound.
A program may use at most 128 MiB of HBM per device.

v0:
```python
import jax
import jax.numpy as jnp
from jax import lax
from jax.sharding import PartitionSpec as P


def with_halo(cells, sides, width):
    for axis, dim in sides:
        count = lax.axis_size(axis)
        ends = count - 1
        head = lax.slice_in_dim(cells, 0, width, axis=dim)
        tail = lax.slice_in_dim(cells, cells.shape[dim] - width, cells.shape[dim], axis=dim)
        cells = jnp.concatenate(
            [
                lax.ppermute(tail, axis, [(i, (i + 1) % count) for i in range(ends)]),
                cells,
                lax.ppermute(head, axis, [((i + 1) % count, i) for i in range(ends)]),
            ],
            axis=dim,
        )
    return cells


def frame_masks(lengths, frames):
    ends = jnp.cumsum(lengths, dtype=jnp.int32)
    starts = ends - lengths
    frame_index = jnp.arange(frames, dtype=jnp.int32)
    inside = (frame_index[:, None] >= starts[None, :]) & (frame_index[:, None] < ends[None, :])
    first = jnp.sum(jnp.where(inside, starts[None, :], 0), axis=1, dtype=jnp.int32)
    return jnp.stack([frame_index - lag >= first for lag in range(3)]).astype(jnp.bfloat16)


def silu_slope(pre, grads):
    sig = jax.nn.sigmoid(pre)
    return grads.astype(jnp.float32) * sig * (1.0 + pre * (1.0 - sig))


def flatten(block):
    return block.reshape(-1, block.shape[-1])


def spatial_forward(padded, weights, cols, rows):
    total = None
    for row_off in range(3):
        for col_off in range(3):
            piece = flatten(padded[col_off : col_off + cols, :, row_off : row_off + rows])
            term = jnp.dot(piece, weights[row_off, col_off], preferred_element_type=jnp.float32)
            total = term if total is None else total + term
    return total


def shards(video, out_grad, lengths, temporal_weight, spatial_weight):
    width_loc = video.shape[1]
    frames = video.shape[2]
    rows = video.shape[3]
    chans = video.shape[4]
    n_tm = lax.axis_size("tm")
    n_height = lax.axis_size("height")
    frames_dev = frames // n_tm
    rows_dev = rows // n_height
    cols_half = out_grad.shape[1]
    total_cols = cols_half * lax.axis_size("width")
    masks = frame_masks(lengths, frames)
    local_video = video[0]
    padded_video = jnp.pad(local_video, ((0, 0), (2, 0), (0, 0), (0, 0)))
    taps = [
        padded_video[:, 2 - lag : 2 - lag + frames] * masks[lag][None, :, None, None]
        for lag in range(3)
    ]
    total = None
    for lag in range(3):
        term = jnp.dot(flatten(taps[lag]), temporal_weight[lag], preferred_element_type=jnp.float32)
        total = term if total is None else total + term
    act_time = total.astype(jnp.bfloat16).reshape(local_video.shape)
    arranged = act_time.reshape(width_loc, n_tm, frames_dev, n_height, rows_dev, chans)
    arranged = arranged.transpose(1, 3, 0, 2, 4, 5).reshape(
        n_tm * n_height * width_loc, frames_dev, rows_dev, chans
    )
    act_space = lax.all_to_all(arranged, ("tm", "height"), split_axis=0, concat_axis=0, tiled=True)
    grad_space = out_grad[0]
    padded_act = with_halo(act_space, (("height", 2), ("width", 0)), 1)
    pre = spatial_forward(padded_act, spatial_weight, cols_half, rows_dev)
    delta = silu_slope(pre, flatten(grad_space)).astype(jnp.bfloat16).reshape(act_space.shape)
    padded_delta = with_halo(delta, (("height", 2), ("width", 0)), 1)
    flat_delta = flatten(delta)
    back = None
    spatial_terms = []
    for row_off in range(3):
        line = []
        for col_off in range(3):
            piece = flatten(
                padded_delta[
                    2 - col_off : 2 - col_off + cols_half, :, 2 - row_off : 2 - row_off + rows_dev
                ]
            )
            term = jnp.dot(
                piece, spatial_weight[row_off, col_off].T, preferred_element_type=jnp.float32
            )
            back = term if back is None else back + term
            source = flatten(
                padded_act[col_off : col_off + cols_half, :, row_off : row_off + rows_dev]
            )
            line.append(
                lax.dot_general(
                    source, flat_delta, (((0,), (0,)), ((), ())), preferred_element_type=jnp.float32
                )
            )
        spatial_terms.append(jnp.stack(line))
    spatial_local = jnp.stack(spatial_terms)
    grad_act_space = back.astype(jnp.bfloat16).reshape(act_space.shape)
    received = lax.all_to_all(
        grad_act_space, ("tm", "height"), split_axis=0, concat_axis=0, tiled=True
    )
    received = received.reshape(n_tm, n_height, width_loc, frames_dev, rows_dev, chans)
    grad_time = received.transpose(2, 0, 3, 1, 4, 5).reshape(width_loc, frames, rows, chans)
    flat_grad = flatten(grad_time)
    frame_total = None
    temporal_terms = []
    for lag in range(3):
        temporal_terms.append(
            lax.dot_general(
                flatten(taps[lag]),
                flat_grad,
                (((0,), (0,)), ((), ())),
                preferred_element_type=jnp.float32,
            )
        )
        masked = flatten(grad_time * masks[lag][None, :, None, None])
        product = jnp.dot(
            masked, temporal_weight[lag].T, preferred_element_type=jnp.float32
        ).reshape(grad_time.shape)
        moved = jnp.pad(product[:, lag:], ((0, 0), (0, lag), (0, 0), (0, 0)))
        frame_total = moved if frame_total is None else frame_total + moved
    temporal_local = jnp.stack(temporal_terms)
    video_grad = frame_total.astype(jnp.bfloat16)[None]
    scale = float(frames * rows * total_cols) ** (-0.5)
    temporal_grad, spatial_grad = lax.psum(
        (temporal_local * scale, spatial_local * scale), ("tm", "height", "width")
    )
    return (video_grad, temporal_grad, spatial_grad)


def solution(mesh):
    placed = (
        P("width", ("tm", "height"), None, None, None),
        P("width", None, "tm", "height", None),
        P(),
        P(),
        P(),
    )
    return jax.shard_map(
        shards,
        mesh=mesh,
        in_specs=placed,
        out_specs=(P("width", ("tm", "height"), None, None, None), P(), P()),
        check_vma=False,
    )
```

profile of v0, /device:TPU:2, one launch (start us, length us, event | category | flops | bytes accessed | tf_op | source)
XLA Modules:
  0.0 414.0 jit_solution(14738831127467204281)
XLA Ops:
  7.2 0.9 reduce-window.8
  8.0 0.7 bitcast_subtract_fusion
  8.8 1.4 broadcast_multiply_fusion
  10.6 1.2 copy-done.15
  12.5 0.5 copy-done.11
  13.3 0.4 fusion.2
  14.0 46.1 %all_to_all.10 = bf16[128,2,16,128]{3,2,1,0:T(8,128)(2,1)S(1)} all-to-all(bf16[128,2,16,128]{3,2,1,0:T(8,128)(2,1)S(1)} %bitcast.249), channel_id=1, replica_groups=mesh['tm'=8,'height'=16,'width'=2] {'tm','height'}, dimensions={0} | all-to-all | bytes 2097152 | tf_op jit(solution)/shard_map/all_to_all | solution.py:79
  60.2 2.4 collective-permute-start
  62.7 5.5 %collective-permute-start.1 = (bf16[128,2,1,128]{3,2,1,0:T(2,128)(2,1)S(1)}, bf16[128,2,1,128]{3,2,1,0:T(2,128)(2,1)S(1)}, u32[]{:S(2)}, u32[]{:S(2)}) collective-permute-start(bf16[128,2,1,128]{3,2,1,0:T(2,128)(2,1)S(1)} %get-tuple-element.38), channel_id=1, source_target_pairs={{2,0},{4,2},{6,4},{8,6},{10,8},{12,10},{14,12},{16,14},{18,16},{20... | collective-permute-start | bytes 196616 | tf_op jit(solution)/shard_map/ppermute | solution.py:17
  68.5 0.7 collective-permute-done
  69.2 1.5 collective-permute-done.1
  70.7 1.3 collective-permute-start.2
  72.0 1.3 collective-permute-start.3
  73.3 1.0 pad_maximum_fusion.4
  75.1 2.0 maximum_maximum_fusion
  77.1 1.3 fusion.67
  78.9 0.4 convolution_add_fusion.13
  81.5 0.4 convolution_add_fusion.9
  82.0 0.4 convolution_add_fusion.8
  82.4 0.8 copy-done.20
  83.2 1.1 fusion.5
  84.4 1.9 collective-permute-start.4
  86.4 6.6 %collective-permute-start.5 = (bf16[128,2,1,128]{3,2,1,0:T(2,128)(2,1)S(1)}, bf16[128,2,1,128]{3,2,1,0:T(2,128)(2,1)S(1)}, u32[]{:S(2)}, u32[]{:S(2)}) collective-permute-start(bf16[128,2,1,128]{3,2,1,0:T(2,128)(2,1)S(1)} %get-tuple-element.34), channel_id=1, source_target_pairs={{2,0},{4,2},{6,4},{8,6},{10,8},{12,10},{14,12},{16,14},{18,16},{20... | collective-permute-start | bytes 196616 | tf_op jit(solution)/shard_map/ppermute | solution.py:17
  93.0 0.5 convolution_bitcast_fusion.9
  93.5 1.6 collective-permute-done.4
  95.1 1.5 collective-permute-done.5
  96.6 1.3 collective-permute-start.6
  97.9 3.0 collective-permute-start.7
  101.0 1.0 pad_maximum_fusion.2
  102.0 0.4 fusion.30
  102.4 2.0 pad_maximum_fusion.1
  104.4 0.6 fusion.65
  105.1 0.6 fusion.66
  105.7 0.4 convolution_add_fusion.6
  106.2 0.4 convolution_add_fusion.5
  106.6 0.4 convolution_add_fusion.4
  107.0 0.4 convolution_add_fusion.3
  107.5 0.4 fusion.14
  107.9 0.4 convolution_add_fusion.2
  108.3 0.4 convolution_add_fusion.1
  108.8 1.4 fusion.3
  110.2 10.4 %all-to-all-start.1 = ((bf16[128,2,16,128]{3,2,1,0:T(8,128)(2,1)}), bf16[128,2,16,128]{3,2,1,0:T(8,128)(2,1)}, u32[]{:S(2)}, u32[]{:S(2)}) async-start(bf16[128,2,16,128]{3,2,1,0:T(8,128)(2,1)} %bitcast.251), calls=%async_computation.1 | async-start | bytes 2097152 | tf_op jit(solution)/shard_map/all_to_all | solution.py:111
  120.9 1.8 convolution_bitcast_fusion.10
  122.8 0.5 convolution_bitcast_fusion.8
  123.3 0.5 convolution_bitcast_fusion.5
  124.0 0.5 convolution_bitcast_fusion.7
  124.5 0.5 convolution_bitcast_fusion.6
  125.2 0.5 convolution_bitcast_fusion.3
  125.8 0.5 convolution_bitcast_fusion.2
  126.3 0.5 convolution_bitcast_fusion.4
  126.8 0.9 maximum_multiply_fusion
  127.7 23.3 %all-to-all-done.1 = bf16[128,2,16,128]{3,2,1,0:T(8,128)(2,1)} async-done(((bf16[128,2,16,128]{3,2,1,0:T(8,128)(2,1)}), bf16[128,2,16,128]{3,2,1,0:T(8,128)(2,1)}, u32[]{:S(2)}, u32[]{:S(2)}) %all-to-all-start.1) | async-done | bytes 1048608 | tf_op jit(solution)/shard_map/all_to_all | solution.py:111
  150.9 1.5 copy.12
  152.5 0.5 convolution_bitcast_fusion.11
  153.0 0.5 convolution_bitcast_fusion.12
  153.7 0.5 convolution_bitcast_fusion.13
  154.2 0.7 maximum_multiply_fusion.1
  154.9 1.5 bitcast_multiply_fusion.2
  156.4 0.4 convolution_bitcast_fusion.1
  157.1 0.4 convolution_bitcast_fusion
  157.6 1.4 fusion.8
  159.1 244.5 %all-reduce.6.cloned.1.call-done = (f32[3,128,128]{2,1,0:T(8,128)}, f32[3,3,128,128]{3,2,1,0:T(8,128)}) async-done(((f32[3,128,128]{2,1,0:T(8,128)}, f32[3,3,128,128]{3,2,1,0:T(8,128)}), (f32[3,128,128]{2,1,0:T(8,128)}, f32[3,3,128,128]{3,2,1,0:T(8,128)})) %all-reduce.6.cloned.1.call-update) | async-done | bytes 786448 | tf_op jit(solution)/shard_map/psum | solution.py:137
  403.6 1.6 copy.18
  405.2 1.9 copy.19
  (70 shorter events, 7.1 us)
Async XLA Ops:
  7.2 3.1 copy-start.19
  10.2 1.8 copy-start.9
  10.2 1.6 copy-start.15
  12.0 1.0 copy-start.11
  12.0 1.3 copy-start.13
  60.2 9.0 %collective-permute-start = (bf16[128,2,1,128]{3,2,1,0:T(2,128)(2,1)S(1)}, bf16[128,2,1,128]{3,2,1,0:T(2,128)(2,1)S(1)}, u32[]{:S(2)}, u32[]{:S(2)}) collective-permute-start(bf16[128,2,1,128]{3,2,1,0:T(2,128)(2,1)S(1)} %get-tuple-element.37), channel_id=1, source_target_pairs={{0,2},{2,4},{4,6},{6,8},{8,10},{10,12},{12,14},{14,16},{16,18},{18... | collective-permute-start | bytes 196616 | tf_op jit(solution)/shard_map/ppermute | solution.py:15
  62.7 8.0 %collective-permute-start.1 = (bf16[128,2,1,128]{3,2,1,0:T(2,128)(2,1)S(1)}, bf16[128,2,1,128]{3,2,1,0:T(2,128)(2,1)S(1)}, u32[]{:S(2)}, u32[]{:S(2)}) collective-permute-start(bf16[128,2,1,128]{3,2,1,0:T(2,128)(2,1)S(1)} %get-tuple-element.38), channel_id=1, source_target_pairs={{2,0},{4,2},{6,4},{8,6},{10,8},{12,10},{14,12},{16,14},{18,16},{20... | collective-permute-start | bytes 196616 | tf_op jit(solution)/shard_map/ppermute | solution.py:17
  68.5 5.9 %copy-start.18 = (bf16[3,3,128,128]{3,2,1,0:T(8,128)(2,1)S(1)}, bf16[3,3,128,128]{3,2,1,0:T(8,128)(2,1)}, u32[]{:S(2)}) copy-start(bf16[3,3,128,128]{3,2,1,0:T(8,128)(2,1)} %param.9) | copy-start | bytes 884740
  70.7 4.1 collective-permute-start.2
  72.0 3.1 collective-permute-start.3
  74.4 8.0 %copy-start.16 = (bf16[128,2,16,128]{3,2,1,0:T(8,128)(2,1)}, bf16[128,2,16,128]{3,2,1,0:T(8,128)(2,1)S(1)}, u32[]{:S(2)}) copy-start(bf16[128,2,16,128]{3,2,1,0:T(8,128)(2,1)S(1)} %get-tuple-element.35) | copy-start | bytes 3145732
  78.4 1.0 copy-start
  78.5 1.4 copy-start.8
  78.5 1.8 copy-start.6
  78.5 2.2 copy-start.2
  78.5 3.0 copy-start.4
  81.9 1.2 copy-start.20
  84.4 10.6 %collective-permute-start.4 = (bf16[128,2,1,128]{3,2,1,0:T(2,128)(2,1)S(1)}, bf16[128,2,1,128]{3,2,1,0:T(2,128)(2,1)S(1)}, u32[]{:S(2)}, u32[]{:S(2)}) collective-permute-start(bf16[128,2,1,128]{3,2,1,0:T(2,128)(2,1)S(1)} %get-tuple-element.33), channel_id=1, source_target_pairs={{0,2},{2,4},{4,6},{6,8},{8,10},{10,12},{12,14},{14,16},{16,18},{18... | collective-permute-start | bytes 196616 | tf_op jit(solution)/shard_map/ppermute | solution.py:15
  86.4 10.2 %collective-permute-start.5 = (bf16[128,2,1,128]{3,2,1,0:T(2,128)(2,1)S(1)}, bf16[128,2,1,128]{3,2,1,0:T(2,128)(2,1)S(1)}, u32[]{:S(2)}, u32[]{:S(2)}) collective-permute-start(bf16[128,2,1,128]{3,2,1,0:T(2,128)(2,1)S(1)} %get-tuple-element.34), channel_id=1, source_target_pairs={{2,0},{4,2},{6,4},{8,6},{10,8},{12,10},{14,12},{16,14},{18,16},{20... | collective-permute-start | bytes 196616 | tf_op jit(solution)/shard_map/ppermute | solution.py:17
  96.6 5.8 %collective-permute-start.6 = (bf16[1,2,18,128]{3,2,1,0:T(8,128)(2,1)S(1)}, bf16[1,2,18,128]{3,2,1,0:T(8,128)(2,1)S(1)}, u32[]{:S(2)}, u32[]{:S(2)}) collective-permute-start(bf16[1,2,18,128]{3,2,1,0:T(8,128)(2,1)S(1)} %get-tuple-element.22), channel_id=1, source_target_pairs={{1,0},{3,2},{5,4},{7,6},{9,8},{11,10},{13,12},{15,14},{17,16},{19,... | collective-permute-start | bytes 27656 | tf_op jit(solution)/shard_map/ppermute | solution.py:17
  97.9 4.5 %collective-permute-start.7 = (bf16[1,2,18,128]{3,2,1,0:T(8,128)(2,1)S(1)}, bf16[1,2,18,128]{3,2,1,0:T(8,128)(2,1)S(1)}, u32[]{:S(2)}, u32[]{:S(2)}) collective-permute-start(bf16[1,2,18,128]{3,2,1,0:T(8,128)(2,1)S(1)} %get-tuple-element.23), channel_id=1, source_target_pairs={{0,1},{2,3},{4,5},{6,7},{8,9},{10,11},{12,13},{14,15},{16,17},{18,... | collective-permute-start | bytes 27656 | tf_op jit(solution)/shard_map/ppermute | solution.py:15
  110.2 40.7 %all-to-all-start.1 = ((bf16[128,2,16,128]{3,2,1,0:T(8,128)(2,1)}), bf16[128,2,16,128]{3,2,1,0:T(8,128)(2,1)}, u32[]{:S(2)}, u32[]{:S(2)}) async-start(bf16[128,2,16,128]{3,2,1,0:T(8,128)(2,1)} %bitcast.251), calls=%async_computation.1 | async-start | bytes 2097152 | tf_op jit(solution)/shard_map/all_to_all | solution.py:111
  120.6 282.9 %all-reduce.6.cloned.1.call-start = ((), (), s32[]{:S(2)}) async-start(), calls=%async_computation.2 | async-start | bytes 1572864 | tf_op jit(solution)/shard_map/psum | solution.py:137
  120.9 1.9 copy-start.7
  120.9 2.4 copy-start.5
  122.8 1.2 copy-start.3
  124.0 1.2 copy-start.17
  124.5 1.3 copy-start.1
  126.8 25.7 %copy-start.14 = (bf16[1,16,256,128]{3,2,1,0:T(8,128)(2,1)S(1)}, bf16[1,16,256,128]{3,2,1,0:T(8,128)(2,1)}, u32[]{:S(2)}) copy-start(bf16[1,16,256,128]{3,2,1,0:T(8,128)(2,1)} %copy-done.13) | copy-start | bytes 3145732
  150.9 2.0 copy-start.12
  152.5 1.2 copy-start.10
Sparse Core Ops, SparseCore 0:
  155.1 248.4 all-reduce.5
where the time goes:
time: 415 us; the launch traced here: 414 us
  waiting for transfers between devices  273 us (66%)
  blocking collectives  46.1 us (11%)
  starting transfers between devices  34.1 us (8%)
  matrix products  20 us (5%)
  between operations  14.7 us (4%)
  local copies, waits for them, and re-layouts  13.4 us (3%)
  other arithmetic  12.4 us (3%)
    psum x1, waiting for transfers between devices, shards(): lax.psum((temporal_local * scale, spatial_local * scale), ('tm', 'height'...  245 us
    all_to_all x1, blocking collectives, shards(): lax.all_to_all(arranged, ('tm', 'height'), split_axis=0, concat_axis=0, t...  46.1 us
    all_to_all x1, waiting for transfers between devices, shards(): lax.all_to_all(grad_act_space, ('tm', 'height'), split_axis=0, concat_axi...  23.3 us
    ppermute x4, starting transfers between devices, with_halo(): lax.ppermute(head, axis, [((i + 1) % count, i) for i in range(ends)])  14.7 us
    all_to_all x1, starting transfers between devices, shards(): lax.all_to_all(grad_act_space, ('tm', 'height'), split_axis=0, concat_axi...  10.4 us
    ppermute x4, starting transfers between devices, with_halo(): lax.ppermute(tail, axis, [(i, (i + 1) % count) for i in range(ends)])  8.68 us
  transfers between devices with their start and end apart: 10, of which 7 were waited for; matrix products, arithmetic and copies ran while one was open for 3% of the time, Pallas kernels for 0%

commit v1 on v0

--- a/solution.py
+++ b/solution.py
@@ -135,7 +135,7 @@
     video_grad = frame_total.astype(jnp.bfloat16)[None]
     scale = float(frames * rows * total_cols) ** (-0.5)
     temporal_grad, spatial_grad = lax.psum(
-        (temporal_local * scale, spatial_local * scale), ("tm", "height", "width")
+        lax.psum((temporal_local * scale, spatial_local * scale), ("height", "width")), "tm"
     )
     return (video_grad, temporal_grad, spatial_grad)
 

time: 415 us -> 351 us (0.85)
  waiting for transfers between devices: 273 us -> 209 us
    psum x1 -> x2, waiting for transfers between devices: 245 us -> 180 us  [the longest x1 107 us: shards(): lax.psum((temporal_local * scale, spatial_local * scale), ('height', 'wid...]
  transfers between devices with their start and end apart: 10 -> 11, of which waited for: 7 -> 8; matrix products, arithmetic and copies ran while one was open for 3% -> 4% of each run, Pallas kernels for 0% -> 0%
where the time goes in v1:
time: 351 us; the launch traced here: 350 us
  waiting for transfers between devices  209 us (60%)
  blocking collectives  46.1 us (13%)
  starting transfers between devices  34.2 us (10%)
  matrix products  19.9 us (6%)
  between operations  14.7 us (4%)
  local copies, waits for them, and re-layouts  13.5 us (4%)
  other arithmetic  12.4 us (4%)
    psum x1, waiting for transfers between devices, shards(): lax.psum((temporal_local * scale, spatial_local * scale), ('height', 'wid...  107 us
    psum x1, waiting for transfers between devices, shards(): lax.psum(lax.psum((temporal_local * scale, spatial_local * scale), ('heig...  73 us
    all_to_all x1, blocking collectives, shards(): lax.all_to_all(arranged, ('tm', 'height'), split_axis=0, concat_axis=0, t...  46.1 us
    all_to_all x1, waiting for transfers between devices, shards(): lax.all_to_all(grad_act_space, ('tm', 'height'), split_axis=0, concat_axi...  23.3 us
    ppermute x4, starting transfers between devices, with_halo(): lax.ppermute(head, axis, [((i + 1) % count, i) for i in range(ends)])  14.9 us
    all_to_all x1, starting transfers between devices, shards(): lax.all_to_all(grad_act_space, ('tm', 'height'), split_axis=0, concat_axi...  10.4 us
    ppermute x4, starting transfers between devices, with_halo(): lax.ppermute(tail, axis, [(i, (i + 1) % count) for i in range(ends)])  8.68 us
    unnamed x44, local copies, waits for them, and re-layouts  8.11 us
  transfers between devices with their start and end apart: 11, of which 8 were waited for; matrix products, arithmetic and copies ran while one was open for 4% of the time, Pallas kernels for 0%

profile of v1, /device:TPU:2, one launch (start us, length us, event | category | flops | bytes accessed | tf_op | source)
XLA Modules:
  0.0 350.2 jit_solution(6964326142621228393)
XLA Ops:
  7.2 0.9 reduce-window.8
  8.0 0.7 bitcast_subtract_fusion
  8.8 1.4 broadcast_multiply_fusion
  10.6 1.2 copy-done.15
  12.5 0.5 copy-done.11
  14.0 46.1 %all_to_all.10 = bf16[128,2,16,128]{3,2,1,0:T(8,128)(2,1)S(1)} all-to-all(bf16[128,2,16,128]{3,2,1,0:T(8,128)(2,1)S(1)} %bitcast.249), channel_id=1, replica_groups=mesh['tm'=8,'height'=16,'width'=2] {'tm','height'}, dimensions={0} | all-to-all | bytes 2097152 | tf_op jit(solution)/shard_map/all_to_all | solution.py:79
  60.3 2.4 collective-permute-start
  62.7 5.6 %collective-permute-start.1 = (bf16[128,2,1,128]{3,2,1,0:T(2,128)(2,1)S(1)}, bf16[128,2,1,128]{3,2,1,0:T(2,128)(2,1)S(1)}, u32[]{:S(2)}, u32[]{:S(2)}) collective-permute-start(bf16[128,2,1,128]{3,2,1,0:T(2,128)(2,1)S(1)} %get-tuple-element.40), channel_id=1, source_target_pairs={{2,0},{4,2},{6,4},{8,6},{10,8},{12,10},{14,12},{16,14},{18,16},{20... | collective-permute-start | bytes 196616 | tf_op jit(solution)/shard_map/ppermute | solution.py:17
  68.4 0.9 collective-permute-done
  69.2 1.6 collective-permute-done.1
  70.9 1.3 collective-permute-start.2
  72.2 1.3 collective-permute-start.3
  73.5 1.0 pad_maximum_fusion.4
  74.5 0.4 fusion.32
  75.3 2.0 maximum_maximum_fusion
  77.3 1.3 fusion.67
  81.2 0.4 convolution_add_fusion.10
  82.1 0.4 convolution_add_fusion.8
  82.6 0.8 copy-done.20
  83.3 1.1 fusion.5
  84.6 1.9 collective-permute-start.4
  86.5 6.6 %collective-permute-start.5 = (bf16[128,2,1,128]{3,2,1,0:T(2,128)(2,1)S(1)}, bf16[128,2,1,128]{3,2,1,0:T(2,128)(2,1)S(1)}, u32[]{:S(2)}, u32[]{:S(2)}) collective-permute-start(bf16[128,2,1,128]{3,2,1,0:T(2,128)(2,1)S(1)} %get-tuple-element.36), channel_id=1, source_target_pairs={{2,0},{4,2},{6,4},{8,6},{10,8},{12,10},{14,12},{16,14},{18,16},{20... | collective-permute-start | bytes 196616 | tf_op jit(solution)/shard_map/ppermute | solution.py:17
  93.2 0.5 convolution_bitcast_fusion.9
  93.7 1.6 collective-permute-done.4
  95.2 1.5 collective-permute-done.5
  96.8 1.3 collective-permute-start.6
  98.1 3.0 collective-permute-start.7
  101.1 1.0 pad_maximum_fusion.2
  102.2 0.4 fusion.30
  102.6 2.0 pad_maximum_fusion.1
  104.6 0.6 fusion.65
  105.2 0.6 fusion.66
  105.9 0.4 convolution_add_fusion.6
  106.3 0.4 convolution_add_fusion.5
  106.8 0.4 convolution_add_fusion.4
  107.2 0.4 convolution_add_fusion.3
  107.6 0.4 fusion.14
  108.1 0.4 convolution_add_fusion.2
  108.5 0.4 convolution_add_fusion.1
  109.0 1.4 fusion.3
  110.4 10.4 %all-to-all-start.1 = ((bf16[128,2,16,128]{3,2,1,0:T(8,128)(2,1)}), bf16[128,2,16,128]{3,2,1,0:T(8,128)(2,1)}, u32[]{:S(2)}, u32[]{:S(2)}) async-start(bf16[128,2,16,128]{3,2,1,0:T(8,128)(2,1)} %bitcast.251), calls=%async_computation.1 | async-start | bytes 2097152 | tf_op jit(solution)/shard_map/all_to_all | solution.py:111
  121.1 1.8 convolution_bitcast_fusion.10
  123.0 0.5 convolution_bitcast_fusion.8
  123.5 0.5 convolution_bitcast_fusion.5
  124.2 0.5 convolution_bitcast_fusion.7
  124.7 0.5 convolution_bitcast_fusion.6
  125.4 0.5 convolution_bitcast_fusion.3
  126.0 0.5 convolution_bitcast_fusion.2
  126.5 0.5 convolution_bitcast_fusion.4
  127.0 0.9 maximum_multiply_fusion
  127.8 23.3 %all-to-all-done.1 = bf16[128,2,16,128]{3,2,1,0:T(8,128)(2,1)} async-done(((bf16[128,2,16,128]{3,2,1,0:T(8,128)(2,1)}), bf16[128,2,16,128]{3,2,1,0:T(8,128)(2,1)}, u32[]{:S(2)}, u32[]{:S(2)}) %all-to-all-start.1) | async-done | bytes 1048608 | tf_op jit(solution)/shard_map/all_to_all | solution.py:111
  151.1 1.5 copy.12
  152.7 0.5 convolution_bitcast_fusion.11
  153.2 0.5 convolution_bitcast_fusion.12
  153.9 0.5 convolution_bitcast_fusion.13
  154.4 0.7 maximum_multiply_fusion.1
  155.4 107.3 %all-reduce.8.cloned.1.call-done = (f32[3,128,128]{2,1,0:T(8,128)}, f32[3,3,128,128]{3,2,1,0:T(8,128)}) async-done(((f32[3,128,128]{2,1,0:T(8,128)}, f32[3,3,128,128]{3,2,1,0:T(8,128)}), (f32[3,128,128]{2,1,0:T(8,128)}, f32[3,3,128,128]{3,2,1,0:T(8,128)})) %all-reduce.8.cloned.1.call-update) | async-done | bytes 786448 | tf_op jit(solution)/shard_map/psum | solution.py:138
  262.7 1.5 bitcast_multiply_fusion.2
  264.2 0.4 convolution_bitcast_fusion.1
  264.9 0.4 convolution_bitcast_fusion
  265.4 1.4 fusion.8
  266.9 73.0 %all-reduce.10.cloned.1.call-done = (f32[3,128,128]{2,1,0:T(8,128)}, f32[3,3,128,128]{3,2,1,0:T(8,128)}) async-done(((f32[3,128,128]{2,1,0:T(8,128)}, f32[3,3,128,128]{3,2,1,0:T(8,128)}), (f32[3,128,128]{2,1,0:T(8,128)}, f32[3,3,128,128]{3,2,1,0:T(8,128)})) %all-reduce.10.cloned.1.call-update) | async-done | bytes 786448 | tf_op jit(solution)/shard_map/psum | solution.py:137
  339.9 1.6 copy.20
  341.5 1.9 copy.21
  (73 shorter events, 7.6 us)
Async XLA Ops:
  7.2 3.1 copy-start.19
  10.2 1.8 copy-start.9
  10.2 1.6 copy-start.15
  12.0 1.0 copy-start.11
  12.0 1.3 copy-start.13
  60.3 9.0 %collective-permute-start = (bf16[128,2,1,128]{3,2,1,0:T(2,128)(2,1)S(1)}, bf16[128,2,1,128]{3,2,1,0:T(2,128)(2,1)S(1)}, u32[]{:S(2)}, u32[]{:S(2)}) collective-permute-start(bf16[128,2,1,128]{3,2,1,0:T(2,128)(2,1)S(1)} %get-tuple-element.39), channel_id=1, source_target_pairs={{0,2},{2,4},{4,6},{6,8},{8,10},{10,12},{12,14},{14,16},{16,18},{18... | collective-permute-start | bytes 196616 | tf_op jit(solution)/shard_map/ppermute | solution.py:15
  62.7 11.8 %copy-start.18 = (bf16[3,3,128,128]{3,2,1,0:T(8,128)(2,1)S(1)}, bf16[3,3,128,128]{3,2,1,0:T(8,128)(2,1)}, u32[]{:S(2)}) copy-start(bf16[3,3,128,128]{3,2,1,0:T(8,128)(2,1)} %param.9) | copy-start | bytes 884740
  62.7 8.1 %collective-permute-start.1 = (bf16[128,2,1,128]{3,2,1,0:T(2,128)(2,1)S(1)}, bf16[128,2,1,128]{3,2,1,0:T(2,128)(2,1)S(1)}, u32[]{:S(2)}, u32[]{:S(2)}) collective-permute-start(bf16[128,2,1,128]{3,2,1,0:T(2,128)(2,1)S(1)} %get-tuple-element.40), channel_id=1, source_target_pairs={{2,0},{4,2},{6,4},{8,6},{10,8},{12,10},{14,12},{16,14},{18,16},{20... | collective-permute-start | bytes 196616 | tf_op jit(solution)/shard_map/ppermute | solution.py:17
  70.9 4.1 %collective-permute-start.2 = (bf16[1,2,18,128]{3,2,1,0:T(8,128)(2,1)S(1)}, bf16[1,2,18,128]{3,2,1,0:T(8,128)(2,1)S(1)}, u32[]{:S(2)}, u32[]{:S(2)}) collective-permute-start(bf16[1,2,18,128]{3,2,1,0:T(8,128)(2,1)S(1)} %get-tuple-element.28), channel_id=1, source_target_pairs={{0,1},{2,3},{4,5},{6,7},{8,9},{10,11},{12,13},{14,15},{16,17},{18,... | collective-permute-start | bytes 27656 | tf_op jit(solution)/shard_map/ppermute | solution.py:15
  72.2 3.1 collective-permute-start.3
  74.5 8.0 %copy-start.16 = (bf16[128,2,16,128]{3,2,1,0:T(8,128)(2,1)}, bf16[128,2,16,128]{3,2,1,0:T(8,128)(2,1)S(1)}, u32[]{:S(2)}) copy-start(bf16[128,2,16,128]{3,2,1,0:T(8,128)(2,1)S(1)} %get-tuple-element.37) | copy-start | bytes 3145732
  78.6 1.0 copy-start
  78.6 1.4 copy-start.8
  78.6 1.8 copy-start.6
  78.6 2.2 copy-start.2
  78.6 3.0 copy-start.4
  82.1 1.2 copy-start.20
  84.6 10.6 %collective-permute-start.4 = (bf16[128,2,1,128]{3,2,1,0:T(2,128)(2,1)S(1)}, bf16[128,2,1,128]{3,2,1,0:T(2,128)(2,1)S(1)}, u32[]{:S(2)}, u32[]{:S(2)}) collective-permute-start(bf16[128,2,1,128]{3,2,1,0:T(2,128)(2,1)S(1)} %get-tuple-element.35), channel_id=1, source_target_pairs={{0,2},{2,4},{4,6},{6,8},{8,10},{10,12},{12,14},{14,16},{16,18},{18... | collective-permute-start | bytes 196616 | tf_op jit(solution)/shard_map/ppermute | solution.py:15
  86.5 10.2 %collective-permute-start.5 = (bf16[128,2,1,128]{3,2,1,0:T(2,128)(2,1)S(1)}, bf16[128,2,1,128]{3,2,1,0:T(2,128)(2,1)S(1)}, u32[]{:S(2)}, u32[]{:S(2)}) collective-permute-start(bf16[128,2,1,128]{3,2,1,0:T(2,128)(2,1)S(1)} %get-tuple-element.36), channel_id=1, source_target_pairs={{2,0},{4,2},{6,4},{8,6},{10,8},{12,10},{14,12},{16,14},{18,16},{20... | collective-permute-start | bytes 196616 | tf_op jit(solution)/shard_map/ppermute | solution.py:17
  96.8 5.8 %collective-permute-start.6 = (bf16[1,2,18,128]{3,2,1,0:T(8,128)(2,1)S(1)}, bf16[1,2,18,128]{3,2,1,0:T(8,128)(2,1)S(1)}, u32[]{:S(2)}, u32[]{:S(2)}) collective-permute-start(bf16[1,2,18,128]{3,2,1,0:T(8,128)(2,1)S(1)} %get-tuple-element.24), channel_id=1, source_target_pairs={{1,0},{3,2},{5,4},{7,6},{9,8},{11,10},{13,12},{15,14},{17,16},{19,... | collective-permute-start | bytes 27656 | tf_op jit(solution)/shard_map/ppermute | solution.py:17
  98.1 4.5 %collective-permute-start.7 = (bf16[1,2,18,128]{3,2,1,0:T(8,128)(2,1)S(1)}, bf16[1,2,18,128]{3,2,1,0:T(8,128)(2,1)S(1)}, u32[]{:S(2)}, u32[]{:S(2)}) collective-permute-start(bf16[1,2,18,128]{3,2,1,0:T(8,128)(2,1)S(1)} %get-tuple-element.25), channel_id=1, source_target_pairs={{0,1},{2,3},{4,5},{6,7},{8,9},{10,11},{12,13},{14,15},{16,17},{18,... | collective-permute-start | bytes 27656 | tf_op jit(solution)/shard_map/ppermute | solution.py:15
  110.4 40.7 %all-to-all-start.1 = ((bf16[128,2,16,128]{3,2,1,0:T(8,128)(2,1)}), bf16[128,2,16,128]{3,2,1,0:T(8,128)(2,1)}, u32[]{:S(2)}, u32[]{:S(2)}) async-start(bf16[128,2,16,128]{3,2,1,0:T(8,128)(2,1)} %bitcast.251), calls=%async_computation.1 | async-start | bytes 2097152 | tf_op jit(solution)/shard_map/all_to_all | solution.py:111
  120.8 141.9 %all-reduce.8.cloned.1.call-start = ((), (), s32[]{:S(2)}) async-start(), calls=%async_computation.2 | async-start | bytes 1572864 | tf_op jit(solution)/shard_map/psum | solution.py:138
  121.1 1.9 copy-start.7
  121.1 2.4 copy-start.5
  123.0 1.2 copy-start.3
  124.2 1.2 copy-start.17
  124.7 1.3 copy-start.1
  126.9 25.7 %copy-start.14 = (bf16[1,16,256,128]{3,2,1,0:T(8,128)(2,1)S(1)}, bf16[1,16,256,128]{3,2,1,0:T(8,128)(2,1)}, u32[]{:S(2)}) copy-start(bf16[1,16,256,128]{3,2,1,0:T(8,128)(2,1)} %copy-done.13) | copy-start | bytes 3145732
  151.1 2.0 copy-start.12
  152.7 1.2 copy-start.10
  155.1 184.8 %all-reduce.10.cloned.1.call-start = ((), (), s32[]{:S(2)}) async-start(), calls=%async_computation.3 | async-start | bytes 1572864 | tf_op jit(solution)/shard_map/psum | solution.py:137
Sparse Core Ops, SparseCore 0:
  155.2 107.4 all-reduce.7
  265.1 74.6 all-reduce.9
